TPU v7x, 32 devices: a whole 2x2x4 slice. The times are simulated.
32 devices in a mesh: dp: 8 (over z, x), seq: 4 (over y, core).
Axes of the slice: x: 2, y: 2, z: 4, core: 2. Of those that a mesh axis runs over, the one named last changes fastest.
Arguments:
- inputs: bfloat16 [32, 1024, 1024], P('dp', 'seq'), may hold values from -6 to 6
- norm_gain: float32 [1024], replicated, may hold values from 0.1 to 1.9
- norm_shift: float32 [1024], replicated, may hold values from -3 to 3
- qkv_weight: bfloat16 [1024, 3072], replicated, may hold values from -0.1875 to 0.1875
- out_weight: bfloat16 [1024, 1024], replicated, may hold values from -0.75 to 0.75
- up_weight: bfloat16 [1024, 4096], replicated, may hold values from -0.1875 to 0.1875
- up_bias: float32 [4096], replicated, may hold values from -3 to 3
- down_weight: bfloat16 [4096, 1024], replicated, may hold values from -0.09375 to 0.09375
- down_bias: float32 [1024], replicated, may hold values from -3 to 3
- partners: int32 [32], P('dp'), may hold values from 0 to 31, as said below
- families: int32 [32, 1024], P('dp'), may hold values from 0 to 1023, as said below
- cotangent: bfloat16 [32, 1024, 1024], P('dp', 'seq'), may hold values from -6 to 6
Outputs:
- layer_out: bfloat16 [32, 1024, 1024], P('dp', 'seq')
- input_grad: float32 [32, 1024, 1024], P('dp', 'seq')
- gain_grad: float32 [1024], replicated
- shift_grad: float32 [1024], replicated
- qkv_grad: float32 [1024, 3072], P('dp', 'seq')
- out_grad: float32 [1024, 1024], P('dp', 'seq')
- up_grad: float32 [1024, 4096], P('dp', 'seq')
- up_bias_grad: float32 [4096], replicated
- down_grad: float32 [4096, 1024], P('dp', 'seq')
- down_bias_grad: float32 [1024], replicated
Inputs may be any that keep to these rules, and one draw needn't show every extreme that they name: partners pairs the rows of each aligned block of 4 rows two by two: partners[partners[r]] = r, partners[r] != r, and partners[r] lies in the block of r. `families`: family ids never fall along a row and the last position of every row has id 1024 - 1; in each aligned block of 4 rows at least one row is a single group over all 1024 positions.
All inputs are finite; a program needn't handle non-finite values.
Results may differ from a plain program's by a relative error of at most 0.0099.
Values may be sent and summed in bfloat16 or wider, within the bound.
A program may use at most 256 MiB of HBM per device.

v0:
```python
import jax
import jax.numpy as jnp
from jax import lax
from jax.sharding import PartitionSpec as P

HEADS = 16
HEAD_DIM = 64
ROT = 32
EPS = 1e-05


def norm_piece(values, norm_gain, norm_shift):
    row_mean = jnp.mean(values, -1, keepdims=True)
    centered = values - row_mean
    variance = jnp.mean(centered * centered, -1, keepdims=True)
    return centered * lax.rsqrt(variance + EPS) * norm_gain + norm_shift


def rotate(values, places):
    half_rot = ROT // 2
    inverse_freq = 10000.0 ** (-2.0 * jnp.arange(half_rot).astype(jnp.float32) / ROT)
    angles = places.astype(jnp.float32)[:, None] * inverse_freq[None, :]
    cosine_table = jnp.cos(angles)[:, None, :]
    sine_table = jnp.sin(angles)[:, None, :]
    first_half = values[..., :half_rot]
    second_half = values[..., half_rot:ROT]
    return jnp.concatenate(
        [
            first_half * cosine_table - second_half * sine_table,
            second_half * cosine_table + first_half * sine_table,
            values[..., ROT:],
        ],
        -1,
    )


def gelu_piece(values):
    return jax.nn.gelu(values, approximate=True)


def masked_scores(queries, key_rows, family):
    scaling = HEAD_DIM ** (-0.5)
    scores = (
        jnp.einsum("qhd,khd->hqk", queries, key_rows, preferred_element_type=jnp.float32) * scaling
    )
    places = jnp.arange(queries.shape[0])
    allowed = (places[None, :] <= places[:, None]) & (family[:, None] == family[None, :])
    return jnp.where(allowed[None], scores, -1000000000.0)


def forward_row(pieces):
    qkv_rows, family = pieces
    scores = masked_scores(qkv_rows[:, 0], qkv_rows[:, 1], family)
    row_max = jnp.max(scores, -1, keepdims=True)
    weights = jnp.exp(scores - row_max)
    row_total = jnp.sum(weights, -1, keepdims=True)
    prob_low = (weights / row_total).astype(jnp.bfloat16)
    mixed_heads = jnp.einsum(
        "hqk,khd->qhd", prob_low, qkv_rows[:, 2], preferred_element_type=jnp.float32
    )
    return (mixed_heads.astype(jnp.bfloat16), (row_max + jnp.log(row_total))[..., 0])


def backward_row(pieces):
    qkv_rows, family, log_total, d_mixed = pieces
    scaling = HEAD_DIM ** (-0.5)
    queries = qkv_rows[:, 0]
    key_rows = qkv_rows[:, 1]
    value_rows = qkv_rows[:, 2]
    scores = masked_scores(queries, key_rows, family)
    chances = jnp.exp(scores - log_total[..., None])
    d_chances = jnp.einsum("qhd,khd->hqk", d_mixed, value_rows, preferred_element_type=jnp.float32)
    d_scores = (chances * (d_chances - jnp.sum(chances * d_chances, -1, keepdims=True))).astype(
        jnp.bfloat16
    )
    d_value = jnp.einsum(
        "hqk,qhd->khd", chances.astype(jnp.bfloat16), d_mixed, preferred_element_type=jnp.float32
    )
    d_query = (
        jnp.einsum("hqk,khd->qhd", d_scores, key_rows, preferred_element_type=jnp.float32) * scaling
    )
    d_key = (
        jnp.einsum("hqk,qhd->khd", d_scores, queries, preferred_element_type=jnp.float32) * scaling
    )
    return jnp.stack([d_query, d_key, d_value], 1).astype(jnp.bfloat16)


def on_device(
    inputs,
    norm_gain,
    norm_shift,
    qkv_weight,
    out_weight,
    up_weight,
    up_bias,
    down_weight,
    down_bias,
    partners,
    families,
    cotangent,
):
    row_count, place_count, model_width = inputs.shape
    seq_size = lax.axis_size("seq")
    token_count = row_count * place_count
    values = inputs.astype(jnp.float32)
    normed, norm_pull = jax.vjp(norm_piece, values, norm_gain, norm_shift)
    normed_low = normed.astype(jnp.bfloat16).reshape(token_count, model_width)
    raw_qkv = jnp.dot(normed_low, qkv_weight, preferred_element_type=jnp.float32)
    raw_qkv = raw_qkv.reshape(row_count, place_count, 3, HEADS, HEAD_DIM)
    places = lax.axis_index("seq") * place_count + jnp.arange(place_count)

    def rope_piece(raw_values):
        return jnp.stack(
            [
                rotate(raw_values[:, :, 0], places),
                rotate(raw_values[:, :, 1], places),
                raw_values[:, :, 2],
            ],
            2,
        )

    rotated, rope_pull = jax.vjp(rope_piece, raw_qkv)
    outgoing = rotated.astype(jnp.bfloat16).reshape(row_count, place_count, 3, seq_size, -1)
    received = lax.all_to_all(outgoing, "seq", split_axis=3, concat_axis=1, tiled=True)
    full_length = received.shape[1]
    received = received.reshape(row_count, full_length, 3, -1, HEAD_DIM)
    mixed_heads, log_totals = lax.map(forward_row, (received, families))
    group_width = mixed_heads.shape[2] * HEAD_DIM
    returned = lax.all_to_all(
        mixed_heads.reshape(row_count, full_length, 1, group_width),
        "seq",
        split_axis=1,
        concat_axis=2,
        tiled=True,
    )
    heads_low = returned.reshape(token_count, model_width)
    attn_out = jnp.dot(heads_low, out_weight, preferred_element_type=jnp.float32)
    hidden = jnp.dot(normed_low, up_weight, preferred_element_type=jnp.float32) + up_bias
    active, gelu_pull = jax.vjp(gelu_piece, hidden)
    active_low = active.astype(jnp.bfloat16)
    mlp_out = jnp.dot(active_low, down_weight, preferred_element_type=jnp.float32) + down_bias
    layer_out = (
        (values.reshape(token_count, model_width) + attn_out + mlp_out)
        .astype(jnp.bfloat16)
        .reshape(inputs.shape)
    )
    local_rows = partners - lax.axis_index("dp") * row_count
    grad_low = jnp.take(cotangent, local_rows, axis=0).reshape(token_count, model_width)
    down_grad = jnp.einsum("tf,td->fd", active_low, grad_low, preferred_element_type=jnp.float32)
    down_bias_grad = jnp.sum(grad_low.astype(jnp.float32), 0)
    out_grad = jnp.einsum("te,td->ed", heads_low, grad_low, preferred_element_type=jnp.float32)
    d_active = jnp.einsum("td,fd->tf", grad_low, down_weight, preferred_element_type=jnp.float32)
    d_hidden_low = gelu_pull(d_active)[0].astype(jnp.bfloat16)
    up_bias_grad = jnp.sum(d_hidden_low.astype(jnp.float32), 0)
    up_grad = jnp.einsum("td,tf->df", normed_low, d_hidden_low, preferred_element_type=jnp.float32)
    d_heads = jnp.einsum(
        "td,ed->te", grad_low, out_weight, preferred_element_type=jnp.float32
    ).astype(jnp.bfloat16)
    d_heads = d_heads.reshape(row_count, place_count, seq_size, group_width)
    d_heads_split = lax.all_to_all(d_heads, "seq", split_axis=2, concat_axis=1, tiled=True)
    d_heads_split = d_heads_split.reshape(row_count, full_length, -1, HEAD_DIM)
    d_blocks = lax.map(backward_row, (received, families, log_totals, d_heads_split))
    d_blocks = d_blocks.reshape(row_count, full_length, 3, 1, group_width)
    d_rotated = lax.all_to_all(d_blocks, "seq", split_axis=1, concat_axis=3, tiled=True)
    d_rotated = d_rotated.reshape(row_count, place_count, 3, HEADS, HEAD_DIM).astype(jnp.float32)
    d_raw_low = rope_pull(d_rotated)[0].astype(jnp.bfloat16).reshape(token_count, 3 * model_width)
    qkv_grad = jnp.einsum("td,te->de", normed_low, d_raw_low, preferred_element_type=jnp.float32)
    d_normed = jnp.einsum("te,de->td", d_raw_low, qkv_weight, preferred_element_type=jnp.float32)
    d_normed = d_normed + jnp.einsum(
        "tf,df->td", d_hidden_low, up_weight, preferred_element_type=jnp.float32
    )
    d_values, gain_grad, shift_grad = norm_pull(d_normed.reshape(inputs.shape))
    input_grad = grad_low.astype(jnp.float32).reshape(inputs.shape) + d_values
    gain_sum, shift_sum, up_bias_sum, down_bias_sum = lax.psum(
        (gain_grad, shift_grad, up_bias_grad, down_bias_grad), ("dp", "seq")
    )
    partial_sums = (
        lax.psum_scatter(qkv_grad, "seq", scatter_dimension=1, tiled=True),
        lax.psum_scatter(out_grad, "seq", scatter_dimension=1, tiled=True),
        lax.psum_scatter(up_grad, "seq", scatter_dimension=1, tiled=True),
        lax.psum_scatter(down_grad, "seq", scatter_dimension=1, tiled=True),
    )
    qkv_sum, out_sum, up_sum, down_sum = (
        lax.psum_scatter(partial_sums[0], "dp", scatter_dimension=0, tiled=True),
        lax.psum_scatter(partial_sums[1], "dp", scatter_dimension=0, tiled=True),
        lax.psum_scatter(partial_sums[2], "dp", scatter_dimension=0, tiled=True),
        lax.psum_scatter(partial_sums[3], "dp", scatter_dimension=0, tiled=True),
    )
    return (
        layer_out,
        input_grad,
        gain_sum,
        shift_sum,
        qkv_sum,
        out_sum,
        up_sum,
        up_bias_sum,
        down_sum,
        down_bias_sum,
    )


def solution(mesh):
    placed = (
        P("dp", "seq", None),
        P(),
        P(),
        P(),
        P(),
        P(),
        P(),
        P(),
        P(),
        P("dp"),
        P("dp", None),
        P("dp", "seq", None),
    )
    return jax.shard_map(
        on_device,
        mesh=mesh,
        in_specs=placed,
        out_specs=(
            P("dp", "seq", None),
            P("dp", "seq", None),
            P(),
            P(),
            P("dp", "seq"),
            P("dp", "seq"),
            P("dp", "seq"),
            P(),
            P("dp", "seq"),
            P(),
        ),
        check_vma=False,
    )
```

profile of v0, /device:TPU:0, one launch (start us, length us, event | category | flops | bytes accessed | tf_op | source)
XLA Modules:
  0.0 1331.5 jit_solution(15439892296866444212)
XLA Ops:
  18.7 4.5 reshape.390
  26.4 4.7 all-to-all-start.2
  36.0 8.7 copy.107
  48.4 10.8 fusion.39
  78.0 5.8 all-to-all-start
  83.8 4.4 convert_reduce_fusion.1
  92.4 4.4 reshape.391
  96.9 58.3 %all-to-all-done = bf16[4,256,3,4,256]{1,4,0,2,3:T(8,128)(2,1)} async-done(((bf16[4,256,3,4,256]{1,4,0,2,3:T(8,128)(2,1)}), bf16[4,256,3,4,256]{1,4,0,2,3:T(8,128)(2,1)}, u32[]{:S(2)}, u32[]{:S(2)}) %all-to-all-start) | async-done | bytes 6291488 | tf_op jit(solution)/shard_map/all_to_all | solution.py:124
  155.2 10.3 copy.112
  165.4 11.0 reshape.385
  176.4 60.7 %while.22 = (s32[]{:T(128)}, bf16[4,1024,4,64]{1,3,2,0:T(8,128)(2,1)}, f32[4,4,1024]{2,1,0:T(4,128)}, bf16[4,1024,3,4,64]{1,4,3,2,0:T(8,128)(2,1)}, s32[4,1024]{1,0:T(4,128)S(1)}, /*index=5*/s32[]{:T(128)}) while((s32[]{:T(128)}, bf16[4,1024,4,64]{1,3,2,0:T(8,128)(2,1)}, f32[4,4,1024]{2,1,0:T(4,128)}, bf16[4,1024,3,4,64]{1,4,3,2,0:T(8,128)(2,1)}, ...), condition=%wide.region_5.6_spmd, body=%wide.region_2.5_spmd.sunk | while | flops 1127477248 | bytes 59913292 | solution.py:127
  186.0 5.6 fusion.93
  201.2 5.6 fusion.93
  216.3 5.6 fusion.93
  231.5 5.6 fusion.93
  241.4 4.6 all-to-all-start.1
  246.0 208.5 %while.23 = (s32[]{:T(128)}, bf16[4,1024,3,4,64]{1,4,3,2,0:T(8,128)(2,1)}, bf16[4,1024,3,4,64]{1,4,3,2,0:T(8,128)(2,1)}, s32[4,1024]{1,0:T(4,128)S(1)}, f32[4,4,...) while((s32[]{:T(128)}, bf16[4,1024,3,4,64]{1,4,3,2,0:T(8,128)(2,1)}, ...), condition=%wide.region_8.9_spmd, body=%wide.region_6.8_spmd.sunk | while | flops 2731274240 | bytes 196179696 | solution.py:162
  247.6 9.6 fusion.99
  258.5 12.7 multiply_reduce_fusion.5
  271.2 11.9 multiply_convert_fusion.5
  286.6 4.5 fusion.102
  291.2 4.5 fusion.101
  299.7 9.6 fusion.99
  310.6 12.7 multiply_reduce_fusion.5
  323.3 11.9 multiply_convert_fusion.5
  338.7 4.5 fusion.102
  343.2 4.5 fusion.101
  351.8 9.6 fusion.99
  362.7 12.7 multiply_reduce_fusion.5
  375.4 11.9 multiply_convert_fusion.5
  390.8 4.5 fusion.102
  395.4 4.5 fusion.101
  403.9 9.6 fusion.99
  414.8 12.7 multiply_reduce_fusion.5
  427.5 11.9 multiply_convert_fusion.5
  443.0 4.5 fusion.102
  447.5 4.5 fusion.101
  454.5 10.8 copy.118
  465.2 5.2 all-to-all-start.3
  476.3 4.5 fusion.51
  480.8 82.8 %all-to-all-done.3 = bf16[4,1024,3,1,256]{4,0,3,2,1:T(4,128)(2,1)} async-done(((bf16[4,1024,3,1,256]{4,0,3,2,1:T(4,128)(2,1)}), bf16[4,1024,3,1,256]{4,0,3,2,1:T(4,128)(2,1)}, u32[]{:S(2)}, u32[]{:S(2)}) %all-to-all-start.3) | async-done | bytes 6291488 | tf_op jit(solution)/shard_map/all_to_all | solution.py:164
  567.4 6.2 convert_bitcast_fusion
  573.6 12.6 copy.120
  586.2 9.9 fusion.45
  602.5 7.1 add_convert_fusion
  609.6 11.5 copy.121
  621.2 5.0 copy.130
  628.8 9.3 fusion.50
  638.2 18.6 %fusion.48 = f32[1024,4096]{1,0:T(8,128)} fusion(bf16[1024,1024]{1,0:T(8,128)(2,1)} %bitcast.215, bf16[1024,4096]{1,0:T(8,128)(2,1)} %param.21), kind=kOutput, calls=%fused_computation.117 | convolution fusion | flops 8589934592 | bytes 27262976 | tf_op jit(solution)/shard_map/dot_general | solution.py:138
  656.8 26.5 %convert_reduce_fusion = (f32[4096]{0:T(1024)S(1)}, bf16[1024,4096]{1,0:T(8,128)(2,1)}) fusion(f32[1024,4096]{1,0:T(8,128)} %fusion.48, f32[4096]{0:T(1024)S(1)} %copy-done.28, bf16[1024,1024]{1,0:T(8,128)(2,1)} %copy-done.9, bf16[4096,1024]{1,0:T(8,128)(2,1)} %param.23), kind=kOutput, calls=%fused_computation.59 | convolution fusion | flops 8686399488 | bytes 35684352 | tf_op jit(solution)/shard_map/td,fd->tf/dot_general | solution.py:152
  683.3 16.3 %fusion.52 = f32[1024,4096]{1,0:T(8,128)} fusion(bf16[1024,1024]{1,0:T(8,128)(2,1)} %bitcast.216, bf16[1024,4096]{1,0:T(8,128)(2,1)} %get-tuple-element.104), kind=kOutput, calls=%fused_computation.121 | convolution fusion | flops 8589934592 | bytes 27262976 | tf_op jit(solution)/shard_map/td,tf->df/dot_general | solution.py:155
  699.7 20.1 %fusion.43 = f32[4096,1024]{1,0:T(8,128)} fusion(bf16[1024,1024]{1,0:T(8,128)(2,1)} %copy-done.9, f32[1024,4096]{1,0:T(8,128)} %fusion.48, f32[4096]{0:T(1024)S(1)} %copy-done.28), kind=kOutput, calls=%fused_computation.113 | convolution fusion | flops 8631877632 | bytes 35667968 | tf_op jit(solution)/shard_map/tf,td->fd/dot_general | solution.py:149
  720.5 17.9 %reduce-scatter.9.cloned.1.call-done = f32[1024,768]{1,0:T(8,128)} async-done(((f32[1024,3072]{1,0:T(8,128)}), f32[1024,768]{1,0:T(8,128)}) %reduce-scatter.9.cloned.1.call-update) | async-done | bytes 3145744 | tf_op jit(solution)/shard_map/reduce_scatter | solution.py:178
  738.5 128.8 %reduce-scatter.17.cloned.1.call-done = f32[1024,1024]{1,0:T(8,128)} async-done(((f32[1024,4096]{1,0:T(8,128)}), f32[1024,1024]{1,0:T(8,128)}) %reduce-scatter.17.cloned.1.call-update) | async-done | bytes 4194320 | tf_op jit(solution)/shard_map/reduce_scatter | solution.py:180
  867.4 5.9 fusion.47
  873.3 122.5 %reduce-scatter.21.cloned.1.call-done = f32[4096,256]{1,0:T(8,128)} async-done(((f32[4096,1024]{1,0:T(8,128)}), f32[4096,256]{1,0:T(8,128)}) %reduce-scatter.21.cloned.1.call-update) | async-done | bytes 4194320 | tf_op jit(solution)/shard_map/reduce_scatter | solution.py:181
  995.9 19.7 %fusion.38 = bf16[1024,1024]{1,0:T(8,128)(2,1)} fusion(f32[1024,1024]{1,0:T(8,128)} %fusion.47, bf16[4,256,1024]{2,1,0:T(8,128)(2,1)} %param.16, f32[1024]{0:T(1024)S(1)} %copy-done.29, bf16[4096,1024]{1,0:T(8,128)(2,1)} %param.23, f32[1024,4096]{1,0:T(8,128)} %fusion.48, f32[4096]{0:T(1024)S(1)} %copy-done.28), kind=kOutput, calls=%fused_computation.74 | convolution fusion | flops 8637120512 | bytes 33574912 | tf_op jit(solution)/shard_map/dot_general | solution.py:141
  1015.5 10.7 fusion.49
  1026.3 14.2 %fusion.46 = (f32[1024]{0:T(1024)S(1)}, f32[1024,1024]{1,0:T(8,128)S(1)}) fusion(f32[1024,1024]{1,0:T(8,128)S(1)} %fusion.49, bf16[1024,4096]{1,0:T(8,128)(2,1)} %get-tuple-element.104, bf16[1024,4096]{1,0:T(8,128)(2,1)} %param.21), kind=kOutput, calls=%fused_computation.115 | convolution fusion | flops 8592030720 | bytes 25169920 | tf_op jit(solution)/shard_map/tf,df->td/dot_general | solution.py:169
  1043.5 40.4 %all-reduce.9 = (f32[1024]{0:T(1024)}, f32[1024]{0:T(1024)}, f32[4096]{0:T(1024)}, f32[1024]{0:T(1024)}) all-reduce(f32[1024]{0:T(1024)S(1)} %get-tuple-element.73, f32[1024]{0:T(1024)S(1)} %get-tuple-element.130, f32[4096]{0:T(1024)S(1)} %get-tuple-element.103, f32[1024]{0:T(1024)S(1)} %copy-done.26), channel_id=1, replica_groups=mesh['dp'=8,'seq'=4] {'dp','seq'}, use_global_device_ids=true, to_apply=%region_12.13 | all-reduce | flops 7168 | bytes 57344 | tf_op jit(solution)/shard_map/psum | solution.py:174
  1083.9 5.7 convert_add_fusion
  1089.6 51.3 %reduce-scatter.11.cloned.1.call-done = f32[128,768]{1,0:T(8,128)} async-done(((f32[1024,768]{1,0:T(8,128)}), f32[128,768]{1,0:T(8,128)}) %reduce-scatter.11.cloned.1.call-update) | async-done | bytes 393232 | tf_op jit(solution)/shard_map/reduce_scatter | solution.py:184
  1140.9 91.2 %reduce-scatter.19.cloned.1.call-done = f32[128,1024]{1,0:T(8,128)} async-done(((f32[1024,1024]{1,0:T(8,128)}), f32[128,1024]{1,0:T(8,128)}) %reduce-scatter.19.cloned.1.call-update) | async-done | bytes 524304 | tf_op jit(solution)/shard_map/reduce_scatter | solution.py:186
  1232.1 92.3 %reduce-scatter.23.cloned.1.call-done = f32[512,256]{1,0:T(8,128)} async-done(((f32[4096,256]{1,0:T(8,128)}), f32[512,256]{1,0:T(8,128)}) %reduce-scatter.23.cloned.1.call-update) | async-done | bytes 524304 | tf_op jit(solution)/shard_map/reduce_scatter | solution.py:187
  (212 shorter events, 146.3 us)
Async XLA Ops:
  7.2 7.7 copy-start
  13.6 1.3 copy-start.9
  26.4 51.6 %all-to-all-start.2 = ((bf16[4,256,4,256]{3,1,0,2:T(8,128)(2,1)}), bf16[4,256,4,256]{3,1,0,2:T(8,128)(2,1)}, u32[]{:S(2)}, u32[]{:S(2)}) async-start(bf16[4,256,4,256]{3,1,0,2:T(8,128)(2,1)} %copy.116), calls=%async_computation.2 | async-start | bytes 4194304 | tf_op jit(solution)/shard_map/all_to_all | solution.py:160
  33.1 11.6 copy-start.17
  35.4 0.6 copy-start.24
  36.0 8.7 copy-start.20
  36.0 8.7 copy-start.22
  36.0 8.7 copy-start.27
  47.1 1.3 copy-start.10
  69.3 3.2 copy-start.8
  69.5 3.0 copy-start.13
  69.5 3.0 copy-start.15
  72.6 1.6 copy-start.6
  78.0 77.2 %all-to-all-start = ((bf16[4,256,3,4,256]{1,4,0,2,3:T(8,128)(2,1)}), bf16[4,256,3,4,256]{1,4,0,2,3:T(8,128)(2,1)}, u32[]{:S(2)}, u32[]{:S(2)}) async-start(bf16[4,256,3,4,256]{1,4,0,2,3:T(8,128)(2,1)} %copy.127), calls=%async_computation | async-start | bytes 12582912 | tf_op jit(solution)/shard_map/all_to_all | solution.py:124
  165.4 11.0 copy-start.19
  241.4 223.9 %all-to-all-start.1 = ((bf16[4,1024,1,256]{3,0,2,1:T(4,128)(2,1)}), bf16[4,1024,1,256]{3,0,2,1:T(4,128)(2,1)}, u32[]{:S(2)}, u32[]{:S(2)}) async-start(bf16[4,1024,1,256]{3,0,2,1:T(4,128)(2,1)} %copy.113), calls=%async_computation.1 | async-start | bytes 4194304 | tf_op jit(solution)/shard_map/all_to_all | solution.py:129
  247.6 10.9 copy-start.1
  271.2 20.0 %slice-start = ((s8[16777216]{0:T(1024)(128)(4,1)}), s8[4194304]{0:T(1024)(128)(4,1)S(1)}, s32[]{:S(2)}) async-start(s8[16777216]{0:T(1024)(128)(4,1)} %bitcast.198), calls=%async_computation.20 | async-start | bytes 8388608 | tf_op jit(solution)/shard_map/while
  271.2 20.0 %slice-start.1 = ((s8[16777216]{0:T(1024)(128)(4,1)}), s8[4194304]{0:T(1024)(128)(4,1)S(1)}, s32[]{:S(2)}) async-start(s8[16777216]{0:T(1024)(128)(4,1)} %bitcast.198), calls=%async_computation.21 | async-start | bytes 8388608 | tf_op jit(solution)/shard_map/while
  271.2 20.0 %slice-start.2 = ((s8[16777216]{0:T(1024)(128)(4,1)}), s8[4194304]{0:T(1024)(128)(4,1)S(1)}, s32[]{:S(2)}) async-start(s8[16777216]{0:T(1024)(128)(4,1)} %bitcast.198), calls=%async_computation.22 | async-start | bytes 8388608 | tf_op jit(solution)/shard_map/while
  283.1 8.1 slice-start.3
  299.7 10.9 copy-start.1
  323.2 20.0 %slice-start = ((s8[16777216]{0:T(1024)(128)(4,1)}), s8[4194304]{0:T(1024)(128)(4,1)S(1)}, s32[]{:S(2)}) async-start(s8[16777216]{0:T(1024)(128)(4,1)} %bitcast.198), calls=%async_computation.20 | async-start | bytes 8388608 | tf_op jit(solution)/shard_map/while
  323.3 20.0 %slice-start.1 = ((s8[16777216]{0:T(1024)(128)(4,1)}), s8[4194304]{0:T(1024)(128)(4,1)S(1)}, s32[]{:S(2)}) async-start(s8[16777216]{0:T(1024)(128)(4,1)} %bitcast.198), calls=%async_computation.21 | async-start | bytes 8388608 | tf_op jit(solution)/shard_map/while
  323.3 20.0 %slice-start.2 = ((s8[16777216]{0:T(1024)(128)(4,1)}), s8[4194304]{0:T(1024)(128)(4,1)S(1)}, s32[]{:S(2)}) async-start(s8[16777216]{0:T(1024)(128)(4,1)} %bitcast.198), calls=%async_computation.22 | async-start | bytes 8388608 | tf_op jit(solution)/shard_map/while
  335.2 8.1 slice-start.3
  351.8 10.9 copy-start.1
  375.4 20.0 %slice-start = ((s8[16777216]{0:T(1024)(128)(4,1)}), s8[4194304]{0:T(1024)(128)(4,1)S(1)}, s32[]{:S(2)}) async-start(s8[16777216]{0:T(1024)(128)(4,1)} %bitcast.198), calls=%async_computation.20 | async-start | bytes 8388608 | tf_op jit(solution)/shard_map/while
  375.4 20.0 %slice-start.1 = ((s8[16777216]{0:T(1024)(128)(4,1)}), s8[4194304]{0:T(1024)(128)(4,1)S(1)}, s32[]{:S(2)}) async-start(s8[16777216]{0:T(1024)(128)(4,1)} %bitcast.198), calls=%async_computation.21 | async-start | bytes 8388608 | tf_op jit(solution)/shard_map/while
  375.4 20.0 %slice-start.2 = ((s8[16777216]{0:T(1024)(128)(4,1)}), s8[4194304]{0:T(1024)(128)(4,1)S(1)}, s32[]{:S(2)}) async-start(s8[16777216]{0:T(1024)(128)(4,1)} %bitcast.198), calls=%async_computation.22 | async-start | bytes 8388608 | tf_op jit(solution)/shard_map/while
  387.3 8.1 slice-start.3
  403.9 10.9 copy-start.1
  427.5 20.0 %slice-start = ((s8[16777216]{0:T(1024)(128)(4,1)}), s8[4194304]{0:T(1024)(128)(4,1)S(1)}, s32[]{:S(2)}) async-start(s8[16777216]{0:T(1024)(128)(4,1)} %bitcast.198), calls=%async_computation.20 | async-start | bytes 8388608 | tf_op jit(solution)/shard_map/while
  427.5 20.0 %slice-start.1 = ((s8[16777216]{0:T(1024)(128)(4,1)}), s8[4194304]{0:T(1024)(128)(4,1)S(1)}, s32[]{:S(2)}) async-start(s8[16777216]{0:T(1024)(128)(4,1)} %bitcast.198), calls=%async_computation.21 | async-start | bytes 8388608 | tf_op jit(solution)/shard_map/while
  427.5 20.0 %slice-start.2 = ((s8[16777216]{0:T(1024)(128)(4,1)}), s8[4194304]{0:T(1024)(128)(4,1)S(1)}, s32[]{:S(2)}) async-start(s8[16777216]{0:T(1024)(128)(4,1)} %bitcast.198), calls=%async_computation.22 | async-start | bytes 8388608 | tf_op jit(solution)/shard_map/while
  439.4 8.1 slice-start.3
  465.2 98.4 %all-to-all-start.3 = ((bf16[4,1024,3,1,256]{4,0,3,2,1:T(4,128)(2,1)}), bf16[4,1024,3,1,256]{4,0,3,2,1:T(4,128)(2,1)}, u32[]{:S(2)}, u32[]{:S(2)}) async-start(bf16[4,1024,3,1,256]{4,0,3,2,1:T(4,128)(2,1)} %copy.118), calls=%async_computation.3 | async-start | bytes 12582912 | tf_op jit(solution)/shard_map/all_to_all | solution.py:164
  470.5 249.4 %reduce-scatter.13.cloned.1.call-start = ((), (), s32[]{:S(2)}) async-start(), calls=%async_computation.14 | async-start | bytes 5242880 | tf_op jit(solution)/shard_map/reduce_scatter | solution.py:179
  472.8 3.5 copy-start.5
  474.9 1.3 copy-start.12
  480.8 257.6 %reduce-scatter.9.cloned.1.call-start = ((), (), s32[]{:S(2)}) async-start(), calls=%async_computation.12 | async-start | bytes 15728640 | tf_op jit(solution)/shard_map/reduce_scatter | solution.py:178
  596.1 2.8 copy-start.4
  596.1 2.8 copy-start.14
  596.1 2.8 copy-start.16
  621.2 7.6 copy-start.11
  626.2 2.6 copy-start.7
  638.1 18.7 %copy-start.28 = (f32[4096]{0:T(1024)S(1)}, f32[4096]{0:T(1024)}, u32[]{:S(2)}) copy-start(f32[4096]{0:T(1024)} %param.22) | copy-start | bytes 49156
  638.1 229.2 %reduce-scatter.17.cloned.1.call-start = ((), (), s32[]{:S(2)}) async-start(), calls=%async_computation.16 | async-start | bytes 20971520 | tf_op jit(solution)/shard_map/reduce_scatter | solution.py:180
  699.7 296.2 %reduce-scatter.21.cloned.1.call-start = ((), (), s32[]{:S(2)}) async-start(), calls=%async_computation.18 | async-start | bytes 20971520 | tf_op jit(solution)/shard_map/reduce_scatter | solution.py:181
  719.8 369.7 %reduce-scatter.15.cloned.1.call-start = ((), (), s32[]{:S(2)}) async-start(), calls=%async_computation.15 | async-start | bytes 1179648 | tf_op jit(solution)/shard_map/reduce_scatter | solution.py:185
  720.4 420.5 %reduce-scatter.11.cloned.1.call-start = ((), (), s32[]{:S(2)}) async-start(), calls=%async_computation.13 | async-start | bytes 3538944 | tf_op jit(solution)/shard_map/reduce_scatter | solution.py:184
  738.4 493.7 %reduce-scatter.19.cloned.1.call-start = ((), (), s32[]{:S(2)}) async-start(), calls=%async_computation.17 | async-start | bytes 4718592 | tf_op jit(solution)/shard_map/reduce_scatter | solution.py:186
  867.3 457.1 %reduce-scatter.23.cloned.1.call-start = ((), (), s32[]{:S(2)}) async-start(), calls=%async_computation.19 | async-start | bytes 4718592 | tf_op jit(solution)/shard_map/reduce_scatter | solution.py:187
  873.3 122.6 %copy-start.29 = (f32[1024]{0:T(1024)S(1)}, f32[1024]{0:T(1024)}, u32[]{:S(2)}) copy-start(f32[1024]{0:T(1024)} %param.24) | copy-start | bytes 12292
  1026.3 14.2 %copy-start.2 = (bf16[4,256,1024]{2,1,0:T(8,128)(2,1)S(1)}, bf16[4,256,1024]{2,1,0:T(8,128)(2,1)}, u32[]{:S(2)}) copy-start(bf16[4,256,1024]{2,1,0:T(8,128)(2,1)} %param.16) | copy-start | bytes 6291460
  1026.3 14.2 %copy-start.18 = (f32[4,256]{1,0:T(4,128)S(1)}, f32[4,256]{1,0:T(4,128)}, u32[]{:S(2)}) copy-start(f32[4,256]{1,0:T(4,128)} %copy-done.17) | copy-start | bytes 12292
  1026.3 14.2 %copy-start.23 = (f32[1024]{0:T(1024)S(1)}, f32[1024]{0:T(1024)}, u32[]{:S(2)}) copy-start(f32[1024]{0:T(1024)} %param.17) | copy-start | bytes 12292
  1040.5 3.0 copy-start.3
  1040.5 0.9 copy-start.25
  1040.5 0.9 copy-start.21
  1041.5 2.0 copy-start.26
Sparse Core Ops, SparseCore 0:
  480.9 69.5 reduce-scatter.12
  638.2 100.1 reduce-scatter.8
  741.1 126.0 reduce-scatter.16
  869.7 126.0 reduce-scatter.20
  1000.0 63.4 reduce-scatter.14
  1067.6 73.3 reduce-scatter.10
  1145.1 86.9 reduce-scatter.18
  1236.7 87.6 reduce-scatter.22
where the time goes:
time: 1340 us; the launch traced here: 1330 us
  waiting for transfers between devices  646 us (48%)
  matrix products  334 us (25%)
  local copies, waits for them, and re-layouts  152 us (11%)
  other arithmetic  123 us (9%)
  blocking collectives  40.4 us (3%)
  starting transfers between devices  21.1 us (2%)
  between operations  14.8 us (1%)
    reduce_scatter x1, waiting for transfers between devices, on_device(): lax.psum_scatter(up_grad, 'seq', scatter_dimension=1, tiled=True)  129 us
    reduce_scatter x1, waiting for transfers between devices, on_device(): lax.psum_scatter(down_grad, 'seq', scatter_dimension=1, tiled=True)  123 us
    reduce_scatter x1, waiting for transfers between devices, on_device(): lax.psum_scatter(partial_sums[3], 'dp', scatter_dimension=0, tiled=True)  92.3 us
    reduce_scatter x1, waiting for transfers between devices, on_device(): lax.psum_scatter(partial_sums[2], 'dp', scatter_dimension=0, tiled=True)  91.2 us
    all_to_all x1, waiting for transfers between devices, on_device(): lax.all_to_all(d_blocks, 'seq', split_axis=1, concat_axis=3, tiled=True)  82.8 us
    dot_general x8, matrix products, masked_scores(): jnp.einsum('qhd,khd->hqk', queries, key_rows, preferred_element_type=jnp....  62.9 us
    all_to_all x1, waiting for transfers between devices, on_device(): lax.all_to_all(outgoing, 'seq', split_axis=3, concat_axis=1, tiled=True)  58.3 us
    reduce_scatter x1, waiting for transfers between devices, on_device(): lax.psum_scatter(partial_sums[0], 'dp', scatter_dimension=0, tiled=True)  51.3 us
  transfers between devices with their start and end apart: 12, of which 8 were waited for; matrix products, arithmetic and copies ran while one was open for 37% of the time, Pallas kernels for 0%

commit v1 on v0

--- a/solution.py
+++ b/solution.py
@@ -121,7 +121,10 @@
 
     rotated, rope_pull = jax.vjp(rope_piece, raw_qkv)
     outgoing = rotated.astype(jnp.bfloat16).reshape(row_count, place_count, 3, seq_size, -1)
-    received = lax.all_to_all(outgoing, "seq", split_axis=3, concat_axis=1, tiled=True)
+    received = jnp.concatenate(
+        lax.all_to_all(jnp.stack(jnp.split(outgoing, lax.axis_size("seq"), axis=3)), "seq", 0, 0),
+        axis=1,
+    )
     full_length = received.shape[1]
     received = received.reshape(row_count, full_length, 3, -1, HEAD_DIM)
     mixed_heads, log_totals = lax.map(forward_row, (received, families))

time: 1340 us -> 1340 us (level)
  no operation moved by 1% of the time
where the time goes in v1:
time: 1340 us; the launch traced here: 1330 us
  waiting for transfers between devices  646 us (48%)
  matrix products  334 us (25%)
  local copies, waits for them, and re-layouts  148 us (11%)
  other arithmetic  125 us (9%)
  blocking collectives  40.4 us (3%)
  starting transfers between devices  21.1 us (2%)
  between operations  14.9 us (1%)
    reduce_scatter x1, waiting for transfers between devices, on_device(): lax.psum_scatter(up_grad, 'seq', scatter_dimension=1, tiled=True)  129 us
    reduce_scatter x1, waiting for transfers between devices, on_device(): lax.psum_scatter(down_grad, 'seq', scatter_dimension=1, tiled=True)  123 us
    reduce_scatter x1, waiting for transfers between devices, on_device(): lax.psum_scatter(partial_sums[3], 'dp', scatter_dimension=0, tiled=True)  92.5 us
    reduce_scatter x1, waiting for transfers between devices, on_device(): lax.psum_scatter(partial_sums[2], 'dp', scatter_dimension=0, tiled=True)  91.5 us
    all_to_all x1, waiting for transfers between devices, on_device(): lax.all_to_all(d_blocks, 'seq', split_axis=1, concat_axis=3, tiled=True)  82.8 us
    dot_general x8, matrix products, masked_scores(): jnp.einsum('qhd,khd->hqk', queries, key_rows, preferred_element_type=jnp....  62.8 us
    all_to_all x1, waiting for transfers between devices, on_device(): lax.all_to_all(jnp.stack(jnp.split(outgoing, lax.axis_size('seq'), axis=3...  58.3 us
    reduce_scatter x1, waiting for transfers between devices, on_device(): lax.psum_scatter(partial_sums[0], 'dp', scatter_dimension=0, tiled=True)  51.1 us
  transfers between devices with their start and end apart: 12, of which 8 were waited for; matrix products, arithmetic and copies ran while one was open for 37% of the time, Pallas kernels for 0%

profile of v1, /device:TPU:0, one launch (start us, length us, event | category | flops | bytes accessed | tf_op | source)
XLA Modules:
  0.0 1330.8 jit_solution(2190498893878276495)
XLA Ops:
  18.6 4.5 reshape.389
  26.4 4.7 all-to-all-start.2
  36.0 8.7 copy.120
  48.4 10.8 fusion.39
  77.3 5.8 all-to-all-start
  83.1 4.4 convert_reduce_fusion.1
  91.7 4.4 reshape.390
  96.1 58.3 %all-to-all-done = bf16[4,4,256,3,1,256]{2,5,1,3,4,0:T(8,128)(2,1)} async-done(((bf16[4,4,256,3,1,256]{2,5,1,3,4,0:T(8,128)(2,1)}), bf16[4,4,256,3,1,256]{2,5,1,3,4,0:T(8,128)(2,1)}, u32[]{:S(2)}, u32[]{:S(2)}) %all-to-all-start) | async-done | bytes 6291488 | tf_op jit(solution)/shard_map/all_to_all | solution.py:125
  154.4 10.3 copy.125
  164.7 11.0 reshape_reshape.3
  175.7 60.7 %while.22 = (s32[]{:T(128)}, bf16[4,1024,4,64]{1,3,2,0:T(8,128)(2,1)}, f32[4,4,1024]{2,1,0:T(4,128)}, bf16[4,1024,3,4,64]{1,4,3,2,0:T(8,128)(2,1)}, s32[4,1024]{1,0:T(4,128)S(1)}, /*index=5*/s32[]{:T(128)}) while((s32[]{:T(128)}, bf16[4,1024,4,64]{1,3,2,0:T(8,128)(2,1)}, f32[4,4,1024]{2,1,0:T(4,128)}, bf16[4,1024,3,4,64]{1,4,3,2,0:T(8,128)(2,1)}, ...), condition=%wide.region_5.6_spmd, body=%wide.region_2.5_spmd.sunk | while | flops 1127477248 | bytes 59913292 | solution.py:130
  185.2 5.6 fusion.93
  200.4 5.6 fusion.93
  215.6 5.6 fusion.93
  230.8 5.6 fusion.93
  240.6 4.6 all-to-all-start.1
  245.3 208.4 %while.23 = (s32[]{:T(128)}, bf16[4,1024,3,4,64]{1,4,3,2,0:T(8,128)(2,1)}, bf16[4,1024,3,4,64]{1,4,3,2,0:T(8,128)(2,1)}, s32[4,1024]{1,0:T(4,128)S(1)}, f32[4,4,...) while((s32[]{:T(128)}, bf16[4,1024,3,4,64]{1,4,3,2,0:T(8,128)(2,1)}, ...), condition=%wide.region_8.9_spmd, body=%wide.region_6.8_spmd.sunk | while | flops 2731274240 | bytes 196179696 | solution.py:165
  246.8 9.6 fusion.99
  257.7 12.7 multiply_reduce_fusion.5
  270.4 11.9 multiply_convert_fusion.5
  285.9 4.5 fusion.102
  290.4 4.5 fusion.101
  298.9 9.6 fusion.99
  309.8 12.7 multiply_reduce_fusion.5
  322.5 11.9 multiply_convert_fusion.5
  338.0 4.5 fusion.102
  342.5 4.5 fusion.101
  351.0 9.6 fusion.99
  361.9 12.7 multiply_reduce_fusion.5
  374.6 11.9 multiply_convert_fusion.5
  390.1 4.5 fusion.102
  394.6 4.5 fusion.101
  403.1 9.6 fusion.99
  414.0 12.7 multiply_reduce_fusion.5
  426.7 11.9 multiply_convert_fusion.5
  442.2 4.5 fusion.102
  446.7 4.5 fusion.101
  453.7 10.8 copy.131
  464.5 5.2 all-to-all-start.3
  475.5 4.5 fusion.51
  480.1 82.8 %all-to-all-done.3 = bf16[4,1024,3,1,256]{4,0,3,2,1:T(4,128)(2,1)} async-done(((bf16[4,1024,3,1,256]{4,0,3,2,1:T(4,128)(2,1)}), bf16[4,1024,3,1,256]{4,0,3,2,1:T(4,128)(2,1)}, u32[]{:S(2)}, u32[]{:S(2)}) %all-to-all-start.3) | async-done | bytes 6291488 | tf_op jit(solution)/shard_map/all_to_all | solution.py:167
  566.6 6.2 convert_bitcast_fusion
  572.8 12.6 copy.133
  585.4 9.9 fusion.45
  601.7 7.1 add_convert_fusion
  608.8 11.5 copy.134
  620.4 5.0 copy.145
  628.0 9.1 fusion.50
  637.2 18.6 %fusion.48 = f32[1024,4096]{1,0:T(8,128)} fusion(bf16[1024,1024]{1,0:T(8,128)(2,1)} %bitcast.227, bf16[1024,4096]{1,0:T(8,128)(2,1)} %param.21), kind=kOutput, calls=%fused_computation.122 | convolution fusion | flops 8589934592 | bytes 27262976 | tf_op jit(solution)/shard_map/dot_general | solution.py:141
  655.9 26.3 %convert_reduce_fusion = (f32[4096]{0:T(1024)S(1)}, bf16[1024,4096]{1,0:T(8,128)(2,1)}) fusion(f32[1024,4096]{1,0:T(8,128)} %fusion.48, f32[4096]{0:T(1024)S(1)} %copy-done.28, bf16[1024,1024]{1,0:T(8,128)(2,1)} %copy-done.9, bf16[4096,1024]{1,0:T(8,128)(2,1)} %param.23), kind=kOutput, calls=%fused_computation.59 | convolution fusion | flops 8686399488 | bytes 35684352 | tf_op jit(solution)/shard_map/td,fd->tf/dot_general | solution.py:155
  682.2 16.3 %fusion.52 = f32[1024,4096]{1,0:T(8,128)} fusion(bf16[1024,1024]{1,0:T(8,128)(2,1)} %bitcast.228, bf16[1024,4096]{1,0:T(8,128)(2,1)} %get-tuple-element.104), kind=kOutput, calls=%fused_computation.126 | convolution fusion | flops 8589934592 | bytes 27262976 | tf_op jit(solution)/shard_map/td,tf->df/dot_general | solution.py:158
  698.6 20.1 %fusion.43 = f32[4096,1024]{1,0:T(8,128)} fusion(bf16[1024,1024]{1,0:T(8,128)(2,1)} %copy-done.9, f32[1024,4096]{1,0:T(8,128)} %fusion.48, f32[4096]{0:T(1024)S(1)} %copy-done.28), kind=kOutput, calls=%fused_computation.118 | convolution fusion | flops 8631877632 | bytes 35667968 | tf_op jit(solution)/shard_map/tf,td->fd/dot_general | solution.py:152
  719.4 18.1 %reduce-scatter.9.cloned.1.call-done = f32[1024,768]{1,0:T(8,128)} async-done(((f32[1024,3072]{1,0:T(8,128)}), f32[1024,768]{1,0:T(8,128)}) %reduce-scatter.9.cloned.1.call-update) | async-done | bytes 3145744 | tf_op jit(solution)/shard_map/reduce_scatter | solution.py:181
  737.5 128.8 %reduce-scatter.17.cloned.1.call-done = f32[1024,1024]{1,0:T(8,128)} async-done(((f32[1024,4096]{1,0:T(8,128)}), f32[1024,1024]{1,0:T(8,128)}) %reduce-scatter.17.cloned.1.call-update) | async-done | bytes 4194320 | tf_op jit(solution)/shard_map/reduce_scatter | solution.py:183
  866.4 5.9 fusion.47
  872.4 122.6 %reduce-scatter.21.cloned.1.call-done = f32[4096,256]{1,0:T(8,128)} async-done(((f32[4096,1024]{1,0:T(8,128)}), f32[4096,256]{1,0:T(8,128)}) %reduce-scatter.21.cloned.1.call-update) | async-done | bytes 4194320 | tf_op jit(solution)/shard_map/reduce_scatter | solution.py:184
  995.0 19.7 %fusion.38 = bf16[1024,1024]{1,0:T(8,128)(2,1)} fusion(f32[1024,1024]{1,0:T(8,128)} %fusion.47, bf16[4,256,1024]{2,1,0:T(8,128)(2,1)} %param.16, f32[1024]{0:T(1024)S(1)} %copy-done.29, bf16[4096,1024]{1,0:T(8,128)(2,1)} %param.23, f32[1024,4096]{1,0:T(8,128)} %fusion.48, f32[4096]{0:T(1024)S(1)} %copy-done.28), kind=kOutput, calls=%fused_computation.75 | convolution fusion | flops 8637120512 | bytes 33574912 | tf_op jit(solution)/shard_map/dot_general | solution.py:144
  1014.6 10.7 fusion.49
  1025.4 14.2 %fusion.46 = (f32[1024]{0:T(1024)S(1)}, f32[1024,1024]{1,0:T(8,128)S(1)}) fusion(f32[1024,1024]{1,0:T(8,128)S(1)} %fusion.49, bf16[1024,4096]{1,0:T(8,128)(2,1)} %get-tuple-element.104, bf16[1024,4096]{1,0:T(8,128)(2,1)} %param.21), kind=kOutput, calls=%fused_computation.120 | convolution fusion | flops 8592030720 | bytes 25169920 | tf_op jit(solution)/shard_map/tf,df->td/dot_general | solution.py:172
  1042.6 40.4 %all-reduce.9 = (f32[1024]{0:T(1024)}, f32[1024]{0:T(1024)}, f32[4096]{0:T(1024)}, f32[1024]{0:T(1024)}) all-reduce(f32[1024]{0:T(1024)S(1)} %get-tuple-element.73, f32[1024]{0:T(1024)S(1)} %get-tuple-element.134, f32[4096]{0:T(1024)S(1)} %get-tuple-element.103, f32[1024]{0:T(1024)S(1)} %copy-done.26), channel_id=1, replica_groups=mesh['dp'=8,'seq'=4] {'dp','seq'}, use_global_device_ids=true, to_apply=%region_12.13 | all-reduce | flops 7168 | bytes 57344 | tf_op jit(solution)/shard_map/psum | solution.py:177
  1083.0 5.7 convert_add_fusion
  1088.7 51.1 %reduce-scatter.11.cloned.1.call-done = f32[128,768]{1,0:T(8,128)} async-done(((f32[1024,768]{1,0:T(8,128)}), f32[128,768]{1,0:T(8,128)}) %reduce-scatter.11.cloned.1.call-update) | async-done | bytes 393232 | tf_op jit(solution)/shard_map/reduce_scatter | solution.py:187
  1139.8 91.5 %reduce-scatter.19.cloned.1.call-done = f32[128,1024]{1,0:T(8,128)} async-done(((f32[1024,1024]{1,0:T(8,128)}), f32[128,1024]{1,0:T(8,128)}) %reduce-scatter.19.cloned.1.call-update) | async-done | bytes 524304 | tf_op jit(solution)/shard_map/reduce_scatter | solution.py:189
  1231.3 92.5 %reduce-scatter.23.cloned.1.call-done = f32[512,256]{1,0:T(8,128)} async-done(((f32[4096,256]{1,0:T(8,128)}), f32[512,256]{1,0:T(8,128)}) %reduce-scatter.23.cloned.1.call-update) | async-done | bytes 524304 | tf_op jit(solution)/shard_map/reduce_scatter | solution.py:190
  (213 shorter events, 145.5 us)
Async XLA Ops:
  7.2 7.7 copy-start
  13.6 1.3 copy-start.9
  26.4 50.9 %all-to-all-start.2 = ((bf16[4,256,4,256]{3,1,0,2:T(8,128)(2,1)}), bf16[4,256,4,256]{3,1,0,2:T(8,128)(2,1)}, u32[]{:S(2)}, u32[]{:S(2)}) async-start(bf16[4,256,4,256]{3,1,0,2:T(8,128)(2,1)} %copy.129), calls=%async_computation.2 | async-start | bytes 4194304 | tf_op jit(solution)/shard_map/all_to_all | solution.py:163
  33.1 11.6 copy-start.17
  35.4 0.6 copy-start.24
  36.0 8.7 copy-start.20
  36.0 8.7 copy-start.22
  36.0 8.7 copy-start.27
  47.1 1.3 copy-start.10
  64.8 3.8 copy-start.5
  68.6 2.3 copy-start.13
  68.6 2.3 copy-start.15
  70.9 1.6 copy-start.7
  77.3 77.2 %all-to-all-start = ((bf16[4,4,256,3,1,256]{2,5,1,3,4,0:T(8,128)(2,1)}), bf16[4,4,256,3,1,256]{2,5,1,3,4,0:T(8,128)(2,1)}, u32[]{:S(2)}, u32[]{:S(2)}) async-start(bf16[4,4,256,3,1,256]{2,5,1,3,4,0:T(8,128)(2,1)} %pad_maximum_fusion.1), calls=%async_computation | async-start | bytes 12582912 | tf_op jit(solution)/shard_map/all_to_all | solution.py:125
  164.7 11.0 copy-start.19
  240.6 223.8 %all-to-all-start.1 = ((bf16[4,1024,1,256]{3,0,2,1:T(4,128)(2,1)}), bf16[4,1024,1,256]{3,0,2,1:T(4,128)(2,1)}, u32[]{:S(2)}, u32[]{:S(2)}) async-start(bf16[4,1024,1,256]{3,0,2,1:T(4,128)(2,1)} %copy.126), calls=%async_computation.1 | async-start | bytes 4194304 | tf_op jit(solution)/shard_map/all_to_all | solution.py:132
  246.8 10.9 copy-start.1
  270.4 20.0 %slice-start = ((s8[16777216]{0:T(1024)(128)(4,1)}), s8[4194304]{0:T(1024)(128)(4,1)S(1)}, s32[]{:S(2)}) async-start(s8[16777216]{0:T(1024)(128)(4,1)} %bitcast.210), calls=%async_computation.20 | async-start | bytes 8388608 | tf_op jit(solution)/shard_map/while
  270.4 20.0 %slice-start.1 = ((s8[16777216]{0:T(1024)(128)(4,1)}), s8[4194304]{0:T(1024)(128)(4,1)S(1)}, s32[]{:S(2)}) async-start(s8[16777216]{0:T(1024)(128)(4,1)} %bitcast.210), calls=%async_computation.21 | async-start | bytes 8388608 | tf_op jit(solution)/shard_map/while
  270.4 20.0 %slice-start.2 = ((s8[16777216]{0:T(1024)(128)(4,1)}), s8[4194304]{0:T(1024)(128)(4,1)S(1)}, s32[]{:S(2)}) async-start(s8[16777216]{0:T(1024)(128)(4,1)} %bitcast.210), calls=%async_computation.22 | async-start | bytes 8388608 | tf_op jit(solution)/shard_map/while
  282.3 8.1 slice-start.3
  298.9 10.9 copy-start.1
  322.5 20.0 %slice-start = ((s8[16777216]{0:T(1024)(128)(4,1)}), s8[4194304]{0:T(1024)(128)(4,1)S(1)}, s32[]{:S(2)}) async-start(s8[16777216]{0:T(1024)(128)(4,1)} %bitcast.210), calls=%async_computation.20 | async-start | bytes 8388608 | tf_op jit(solution)/shard_map/while
  322.5 20.0 %slice-start.1 = ((s8[16777216]{0:T(1024)(128)(4,1)}), s8[4194304]{0:T(1024)(128)(4,1)S(1)}, s32[]{:S(2)}) async-start(s8[16777216]{0:T(1024)(128)(4,1)} %bitcast.210), calls=%async_computation.21 | async-start | bytes 8388608 | tf_op jit(solution)/shard_map/while
  322.5 20.0 %slice-start.2 = ((s8[16777216]{0:T(1024)(128)(4,1)}), s8[4194304]{0:T(1024)(128)(4,1)S(1)}, s32[]{:S(2)}) async-start(s8[16777216]{0:T(1024)(128)(4,1)} %bitcast.210), calls=%async_computation.22 | async-start | bytes 8388608 | tf_op jit(solution)/shard_map/while
  334.4 8.1 slice-start.3
  351.0 10.9 copy-start.1
  374.6 20.0 %slice-start = ((s8[16777216]{0:T(1024)(128)(4,1)}), s8[4194304]{0:T(1024)(128)(4,1)S(1)}, s32[]{:S(2)}) async-start(s8[16777216]{0:T(1024)(128)(4,1)} %bitcast.210), calls=%async_computation.20 | async-start | bytes 8388608 | tf_op jit(solution)/shard_map/while
  374.6 20.0 %slice-start.1 = ((s8[16777216]{0:T(1024)(128)(4,1)}), s8[4194304]{0:T(1024)(128)(4,1)S(1)}, s32[]{:S(2)}) async-start(s8[16777216]{0:T(1024)(128)(4,1)} %bitcast.210), calls=%async_computation.21 | async-start | bytes 8388608 | tf_op jit(solution)/shard_map/while
  374.6 20.0 %slice-start.2 = ((s8[16777216]{0:T(1024)(128)(4,1)}), s8[4194304]{0:T(1024)(128)(4,1)S(1)}, s32[]{:S(2)}) async-start(s8[16777216]{0:T(1024)(128)(4,1)} %bitcast.210), calls=%async_computation.22 | async-start | bytes 8388608 | tf_op jit(solution)/shard_map/while
  386.5 8.1 slice-start.3
  403.1 10.9 copy-start.1
  426.7 20.0 %slice-start = ((s8[16777216]{0:T(1024)(128)(4,1)}), s8[4194304]{0:T(1024)(128)(4,1)S(1)}, s32[]{:S(2)}) async-start(s8[16777216]{0:T(1024)(128)(4,1)} %bitcast.210), calls=%async_computation.20 | async-start | bytes 8388608 | tf_op jit(solution)/shard_map/while
  426.7 20.0 %slice-start.1 = ((s8[16777216]{0:T(1024)(128)(4,1)}), s8[4194304]{0:T(1024)(128)(4,1)S(1)}, s32[]{:S(2)}) async-start(s8[16777216]{0:T(1024)(128)(4,1)} %bitcast.210), calls=%async_computation.21 | async-start | bytes 8388608 | tf_op jit(solution)/shard_map/while
  426.7 20.0 %slice-start.2 = ((s8[16777216]{0:T(1024)(128)(4,1)}), s8[4194304]{0:T(1024)(128)(4,1)S(1)}, s32[]{:S(2)}) async-start(s8[16777216]{0:T(1024)(128)(4,1)} %bitcast.210), calls=%async_computation.22 | async-start | bytes 8388608 | tf_op jit(solution)/shard_map/while
  438.6 8.1 slice-start.3
  464.5 98.4 %all-to-all-start.3 = ((bf16[4,1024,3,1,256]{4,0,3,2,1:T(4,128)(2,1)}), bf16[4,1024,3,1,256]{4,0,3,2,1:T(4,128)(2,1)}, u32[]{:S(2)}, u32[]{:S(2)}) async-start(bf16[4,1024,3,1,256]{4,0,3,2,1:T(4,128)(2,1)} %copy.131), calls=%async_computation.3 | async-start | bytes 12582912 | tf_op jit(solution)/shard_map/all_to_all | solution.py:167
  469.7 249.1 %reduce-scatter.13.cloned.1.call-start = ((), (), s32[]{:S(2)}) async-start(), calls=%async_computation.14 | async-start | bytes 5242880 | tf_op jit(solution)/shard_map/reduce_scatter | solution.py:182
  472.0 3.5 copy-start.6
  474.2 1.3 copy-start.12
  480.0 257.4 %reduce-scatter.9.cloned.1.call-start = ((), (), s32[]{:S(2)}) async-start(), calls=%async_computation.12 | async-start | bytes 15728640 | tf_op jit(solution)/shard_map/reduce_scatter | solution.py:181
  595.3 2.8 copy-start.4
  595.3 2.8 copy-start.14
  595.4 2.8 copy-start.16
  620.4 7.6 copy-start.11
  625.4 2.6 copy-start.8
  637.1 18.7 %copy-start.28 = (f32[4096]{0:T(1024)S(1)}, f32[4096]{0:T(1024)}, u32[]{:S(2)}) copy-start(f32[4096]{0:T(1024)} %param.22) | copy-start | bytes 49156
  637.2 229.2 %reduce-scatter.17.cloned.1.call-start = ((), (), s32[]{:S(2)}) async-start(), calls=%async_computation.16 | async-start | bytes 20971520 | tf_op jit(solution)/shard_map/reduce_scatter | solution.py:183
  698.5 296.4 %reduce-scatter.21.cloned.1.call-start = ((), (), s32[]{:S(2)}) async-start(), calls=%async_computation.18 | async-start | bytes 20971520 | tf_op jit(solution)/shard_map/reduce_scatter | solution.py:184
  718.7 370.0 %reduce-scatter.15.cloned.1.call-start = ((), (), s32[]{:S(2)}) async-start(), calls=%async_computation.15 | async-start | bytes 1179648 | tf_op jit(solution)/shard_map/reduce_scatter | solution.py:188
  719.3 420.5 %reduce-scatter.11.cloned.1.call-start = ((), (), s32[]{:S(2)}) async-start(), calls=%async_computation.13 | async-start | bytes 3538944 | tf_op jit(solution)/shard_map/reduce_scatter | solution.py:187
  737.5 493.8 %reduce-scatter.19.cloned.1.call-start = ((), (), s32[]{:S(2)}) async-start(), calls=%async_computation.17 | async-start | bytes 4718592 | tf_op jit(solution)/shard_map/reduce_scatter | solution.py:189
  866.4 457.4 %reduce-scatter.23.cloned.1.call-start = ((), (), s32[]{:S(2)}) async-start(), calls=%async_computation.19 | async-start | bytes 4718592 | tf_op jit(solution)/shard_map/reduce_scatter | solution.py:190
  872.3 122.6 %copy-start.29 = (f32[1024]{0:T(1024)S(1)}, f32[1024]{0:T(1024)}, u32[]{:S(2)}) copy-start(f32[1024]{0:T(1024)} %param.24) | copy-start | bytes 12292
  1025.4 14.2 %copy-start.2 = (bf16[4,256,1024]{2,1,0:T(8,128)(2,1)S(1)}, bf16[4,256,1024]{2,1,0:T(8,128)(2,1)}, u32[]{:S(2)}) copy-start(bf16[4,256,1024]{2,1,0:T(8,128)(2,1)} %param.16) | copy-start | bytes 6291460
  1025.4 14.2 %copy-start.18 = (f32[4,256]{1,0:T(4,128)S(1)}, f32[4,256]{1,0:T(4,128)}, u32[]{:S(2)}) copy-start(f32[4,256]{1,0:T(4,128)} %copy-done.17) | copy-start | bytes 12292
  1025.4 14.2 %copy-start.23 = (f32[1024]{0:T(1024)S(1)}, f32[1024]{0:T(1024)}, u32[]{:S(2)}) copy-start(f32[1024]{0:T(1024)} %param.17) | copy-start | bytes 12292
  1039.6 3.0 copy-start.3
  1039.6 0.9 copy-start.25
  1039.6 0.9 copy-start.21
  1040.6 2.0 copy-start.26
Sparse Core Ops, SparseCore 0:
  480.1 69.5 reduce-scatter.12
  637.3 100.1 reduce-scatter.8
  740.2 126.0 reduce-scatter.16
  868.8 126.1 reduce-scatter.20
  999.1 63.3 reduce-scatter.14
  1066.6 73.1 reduce-scatter.10
  1144.0 87.2 reduce-scatter.18
  1235.9 87.7 reduce-scatter.22
